TPU v7x, 256 devices: a whole 4x4x8 slice. The times are simulated.
256 devices in a mesh: tm: 4 (over y), det: 64 (over z, x, core).
Axes of the slice: x: 4, y: 4, z: 8, core: 2. Of those that a mesh axis runs over, the one named last changes fastest.
Arguments:
- offset_amplitude_array: float32 [128, 16], P('det', 'tm'), may hold values from -6 to 6
- system_remainder: float32 [128, 16], P('det', 'tm'), may hold values from -6 to 6
- conjugate_heading: float32 [128, 16], P('det', 'tm'), may hold values from -6 to 6
- region_cell_numbers: int32 [128, 16384], P('det', 'tm'), may hold values from 0 to 255
- stokes_reading_rotation: float32 [128, 16384], P('det', 'tm'), may hold values from -3.140625 to 3.140625
- scan_patch_places: int32 [128, 128], P('det', 'tm'), may hold values from 0 to 127
- holder_visited_regions: int32 [4, 64, 64, 2], P('tm', 'det'), may hold values from 0 to 47, as said below
- stokes_precision_matrices: float32 [3072, 6, 256], P('det'), as said below
Outputs:
- refreshed_offset_amplitudes: float32 [128, 16], P('det', 'tm')
- updated_residual_vector: float32 [128, 16], P('det', 'tm')
- updated_search_direction: float32 [128, 16], P('det', 'tm')
Inputs may be any that keep to these rules, and one draw needn't show every extreme that they name: For each device (i, j) and owner o, holder_visited_regions[i, j, o, :] holds 2 distinct local submaps. `stokes_precision_matrices`: each pixel's 3x3 block is symmetric positive definite.
All inputs are finite; a program needn't handle non-finite values.
Results may differ from a plain program's by a relative error of at most 0.00005.
Values sent between devices are 32-bit elements; how exact they have to be, the bound alone decides.
No kernel may reach another device: no remote copies, remote signals or barrier semaphores. Data moves between devices by JAX's collectives and lax.ppermute only.
A program may use at most 64 MiB of HBM per device.

v0:
```python
import jax
import jax.numpy as jnp
from jax import lax
from jax.sharding import PartitionSpec as P

TILE = 128
WINDOW = 256
stiffness = 0.5


def extended(value, sides, width):
    for axis, dim in sides:
        peers, length = (lax.axis_size(axis), value.shape[dim])
        up = [(i, (i + 1) % peers) for i in range(peers - 1)]
        down = [(j, i) for i, j in up]
        last = lax.slice_in_dim(value, length - width, length, axis=dim)
        leading = lax.slice_in_dim(value, 0, width, axis=dim)
        before = lax.ppermute(last, axis, up)
        after = lax.ppermute(leading, axis, down)
        value = jnp.concatenate([before, value, after], axis=dim)
    return value


def solve_blocks(binned, stokes_precision_matrices):
    first = binned[:, 0]
    second = binned[:, 1]
    third = binned[:, 2]
    out_first = (
        stokes_precision_matrices[:, 0] * first
        + stokes_precision_matrices[:, 1] * second
        + stokes_precision_matrices[:, 2] * third
    )
    out_second = (
        stokes_precision_matrices[:, 1] * first
        + stokes_precision_matrices[:, 3] * second
        + stokes_precision_matrices[:, 4] * third
    )
    out_third = (
        stokes_precision_matrices[:, 2] * first
        + stokes_precision_matrices[:, 4] * second
        + stokes_precision_matrices[:, 5] * third
    )
    return jnp.stack([out_first, out_second, out_third], axis=1)


def shards(
    offset_amplitude_array,
    system_remainder,
    conjugate_heading,
    region_cell_numbers,
    stokes_reading_rotation,
    scan_patch_places,
    holder_visited_regions,
    stokes_precision_matrices,
):
    det_dev, base_dev = conjugate_heading.shape
    samp_dev = region_cell_numbers.shape[1]
    per_owner = holder_visited_regions.shape[3]
    owners = lax.axis_size("det")
    slot_count = owners * per_owner
    sub_dev = stokes_precision_matrices.shape[0]
    cells = 3 * WINDOW
    stream = jnp.repeat(conjugate_heading, samp_dev // base_dev, axis=1)
    twice = 2.0 * stokes_reading_rotation
    cos_weight = jnp.cos(twice)
    sin_weight = jnp.sin(twice)
    slot_index = jnp.repeat(scan_patch_places, TILE, axis=1)
    cell = slot_index * cells + region_cell_numbers
    values = jnp.concatenate(
        [stream.ravel(), (stream * cos_weight).ravel(), (stream * sin_weight).ravel()]
    )
    targets = jnp.concatenate([cell.ravel(), (cell + WINDOW).ravel(), (cell + 2 * WINDOW).ravel()])
    local_bins = jax.ops.segment_sum(values, targets, num_segments=slot_count * cells).reshape(
        slot_count, cells
    )
    my_hits = holder_visited_regions.reshape(owners, per_owner)
    global_ids = jnp.arange(slot_count, dtype=jnp.int32) // per_owner * sub_dev + my_hits.reshape(
        -1
    )
    selector = (
        global_ids[None, :] == jnp.arange(sub_dev * owners, dtype=jnp.int32)[:, None]
    ).astype(jnp.float32)
    full_bins = jnp.dot(
        selector, local_bins, precision=lax.Precision.HIGHEST, preferred_element_type=jnp.float32
    )
    owned = lax.psum_scatter(full_bins, "det", scatter_dimension=0, tiled=True)
    binned = lax.psum(owned, "tm")
    sky_map = solve_blocks(binned.reshape(sub_dev, 3, WINDOW), stokes_precision_matrices).reshape(
        sub_dev, cells
    )
    whole_sky = lax.all_gather(sky_map, "det", axis=0, tiled=True)
    slot_sky = jnp.dot(
        selector.T, whole_sky, precision=lax.Precision.HIGHEST, preferred_element_type=jnp.float32
    )
    flat_sky = slot_sky.reshape(-1)
    scanned = (
        flat_sky[cell]
        + cos_weight * flat_sky[cell + WINDOW]
        + sin_weight * flat_sky[cell + 2 * WINDOW]
    )
    folded = scanned.reshape(det_dev, base_dev, samp_dev // base_dev).sum(axis=2) / (
        samp_dev // base_dev
    )
    padded = extended(conjugate_heading, (("tm", 1),), 1)
    applied = (
        conjugate_heading
        + folded
        + stiffness * (2.0 * conjugate_heading - padded[:, :-2] - padded[:, 2:])
    )
    norm_now, curvature = lax.psum(
        (jnp.sum(system_remainder * system_remainder), jnp.sum(conjugate_heading * applied)),
        ("tm", "det"),
    )
    conjugate_update_factor = norm_now / curvature
    updated_residual_vector = system_remainder - conjugate_update_factor * applied
    norm_next = lax.psum(jnp.sum(updated_residual_vector * updated_residual_vector), ("tm", "det"))
    refreshed_offset_amplitudes = (
        offset_amplitude_array + conjugate_update_factor * conjugate_heading
    )
    updated_search_direction = updated_residual_vector + norm_next / norm_now * conjugate_heading
    return (refreshed_offset_amplitudes, updated_residual_vector, updated_search_direction)


def solution(mesh):
    return jax.shard_map(
        shards,
        mesh=mesh,
        in_specs=(
            P("det", "tm"),
            P("det", "tm"),
            P("det", "tm"),
            P("det", "tm"),
            P("det", "tm"),
            P("det", "tm"),
            P("tm", "det", None, None),
            P("det", None, None),
        ),
        out_specs=(P("det", "tm"), P("det", "tm"), P("det", "tm")),
        check_vma=False,
    )
```

profile of v0, /device:TPU:1, one launch (start us, length us, event | category | flops | bytes accessed | tf_op | source)
XLA Modules:
  0.0 786.4 jit_solution(1612959436937574905)
XLA Ops:
  7.2 0.0 reduce-scatter.2.cloned.1.call-start
  7.2 0.7 broadcast_multiply_fusion
  7.9 0.1 broadcast_bitcast_fusion.2
  8.0 0.8 fusion.12
  8.9 0.8 broadcast_bitcast_fusion.1
  9.7 1.2 multiply_bitcast_fusion.1
  11.0 169.6 %scatter_custom_fusion = f32[98304]{0:T(1024)S(1)} fusion(s32[24576]{0:T(1024)S(1)} %pad_add_fusion, f32[24576]{0:T(1024)S(1)} %pad_maximum_fusion.1, f32[]{:T(128)} %constant.14.clone.1), kind=kCustom, calls=%fused_computation.10 | custom fusion | flops 24576 | bytes 393220 | tf_op jit(solution)/shard_map/scatter-add | solution.py:73
  180.6 0.1 reshape.67
  180.7 0.8 copy.13
  181.4 0.1 reshape_reshape.6
  181.6 0.0 copy-start
  181.6 6.2 fusion.1
  187.8 0.0 reduce-scatter.2.cloned.1.call-update
  187.8 0.0 all-reduce.3.cloned.1.call-start
  187.9 155.1 %reduce-scatter.2.cloned.1.call-done = f32[48,768]{1,0:T(8,128)} async-done(((f32[3072,768]{1,0:T(8,128)}), f32[48,768]{1,0:T(8,128)}) %reduce-scatter.2.cloned.1.call-update) | async-done | bytes 147472 | tf_op jit(solution)/shard_map/reduce_scatter | solution.py:86
  343.0 1.6 reshape.68
  344.6 0.0 all-reduce.3.cloned.1.call-update
  344.6 0.0 all-gather.2.cloned.1.call-start
  344.7 0.0 copy-done
  344.7 47.9 %all-reduce.3.cloned.1.call-done = f32[48,3,256]{2,1,0:T(4,128)} async-done(((f32[48,3,256]{2,1,0:T(4,128)}), f32[48,3,256]{2,1,0:T(4,128)}) %all-reduce.3.cloned.1.call-update) | async-done | bytes 147472 | tf_op jit(solution)/shard_map/psum | solution.py:87
  392.6 1.4 fusion.10
  394.1 0.1 pad_maximum_fusion
  394.2 0.7 copy.31
  394.9 0.0 all-gather.2.cloned.1.call-update
  394.9 0.0 copy-done.2
  394.9 0.1 fusion.17
  395.0 2.2 collective-permute-start
  397.3 1.3 collective-permute-start.1
  398.6 0.0 collective-permute-done
  398.6 3.0 collective-permute-done.1
  401.6 0.1 pad_maximum_fusion.2
  401.7 80.8 %all-gather.2.cloned.1.call-done = f32[3072,768]{1,0:T(8,128)} async-done(((f32[48,768]{1,0:T(8,128)}), f32[3072,768]{1,0:T(8,128)}) %all-gather.2.cloned.1.call-update) | async-done | bytes 9437200 | tf_op jit(solution)/shard_map/all_gather | solution.py:91
  482.5 7.3 fusion
  489.9 45.5 %gather_fusion = f32[8192]{0:T(1024)S(1)} fusion(f32[98304]{0:T(1024)S(1)} %reshape.70, s32[8192]{0:T(1024)S(1)} %broadcast_clamp_fusion.2), kind=kCustom, calls=%fused_computation | custom fusion | bytes 98304 | tf_op jit(solution)/shard_map/gather | solution.py:97
  535.4 45.5 %gather_fusion.1 = f32[8192]{0:T(1024)S(1)} fusion(f32[98304]{0:T(1024)S(1)} %reshape.70, s32[8192]{0:T(1024)S(1)} %broadcast_clamp_fusion.1), kind=kCustom, calls=%fused_computation.1 | custom fusion | bytes 98304 | tf_op jit(solution)/shard_map/gather | solution.py:98
  581.0 0.0 copy-start.1
  581.0 0.0 copy-start.3
  581.0 0.0 copy-start.5
  581.1 45.5 %gather_fusion.2 = f32[8192]{0:T(1024)S(1)} fusion(f32[98304]{0:T(1024)S(1)} %reshape.70, s32[8192]{0:T(1024)S(1)} %broadcast_clamp_fusion), kind=kCustom, calls=%fused_computation.2 | custom fusion | bytes 98304 | tf_op jit(solution)/shard_map/gather | solution.py:99
  626.6 0.0 copy-done.1
  626.6 0.5 multiply_add_fusion
  627.2 0.1 reduce_sum.37
  627.3 0.7 multiply_reduce_fusion.1
  627.9 74.6 %all-reduce = (f32[]{:T(128)}, f32[]{:T(128)}) all-reduce(f32[]{:T(128)} %get-tuple-element.34, f32[]{:T(128)} %get-tuple-element.7), channel_id=1, replica_groups=mesh['tm'=4,'det'=64] {'tm','det'}, use_global_device_ids=true, to_apply=%region_1.2 | all-reduce | flops 2 | bytes 16 | tf_op jit(solution)/shard_map/psum | solution.py:110
  703.9 0.6 multiply_reduce_fusion
  704.5 73.4 %psum.31 = f32[]{:T(128)} all-reduce(f32[]{:T(128)} %get-tuple-element.5), channel_id=1, replica_groups=mesh['tm'=4,'det'=64] {'tm','det'}, use_global_device_ids=true, to_apply=%region_9.10 | all-reduce | flops 1 | bytes 8 | tf_op jit(solution)/shard_map/psum | solution.py:116
  779.2 0.6 multiply_add_fusion.1
  779.8 0.0 copy-done.4
  (27 shorter events, 0.3 us)
Async XLA Ops:
  7.2 335.8 %reduce-scatter.2.cloned.1.call-start = ((), (), s32[]{:S(2)}) async-start(), calls=%async_computation.1 | async-start | bytes 9584640 | tf_op jit(solution)/shard_map/reduce_scatter | solution.py:86
  181.6 163.1 %copy-start = (f32[48,6,256]{2,0,1:T(8,128)S(1)}, f32[48,6,256]{2,0,1:T(8,128)}, u32[]{:S(2)}) copy-start(f32[48,6,256]{2,0,1:T(8,128)} %param.15) | copy-start | bytes 884740
  187.8 207.2 %copy-start.2 = (f32[2,4]{1,0:T(2,128)S(1)}, f32[2,4]{1,0:T(2,128)}, u32[]{:S(2)}) copy-start(f32[2,4]{1,0:T(2,128)} %param.10) | copy-start | bytes 100
  187.8 204.8 %all-reduce.3.cloned.1.call-start = ((), (), s32[]{:S(2)}) async-start(), calls=%async_computation.2 | async-start | bytes 393216 | tf_op jit(solution)/shard_map/psum | solution.py:87
  344.6 137.9 %all-gather.2.cloned.1.call-start = ((), (), s32[]{:S(2)}) async-start(), calls=%async_computation.3 | async-start | bytes 9584640 | tf_op jit(solution)/shard_map/all_gather | solution.py:91
  395.0 3.6 collective-permute-start
  397.3 4.4 collective-permute-start.1
  581.0 45.6 %copy-start.1 = (f32[2,4096]{1,0:T(2,128)S(1)}, f32[2,4096]{1,0:T(2,128)}, u32[]{:S(2)}) copy-start(f32[2,4096]{1,0:T(2,128)} %param.12) | copy-start | bytes 98308
  581.0 46.2 %copy-start.3 = (f32[2,4]{1,0:T(2,128)S(1)}, f32[2,4]{1,0:T(2,128)}, u32[]{:S(2)}) copy-start(f32[2,4]{1,0:T(2,128)} %param.9) | copy-start | bytes 100
  581.0 198.2 %copy-start.5 = (f32[2,4]{1,0:T(2,128)S(1)}, f32[2,4]{1,0:T(2,128)}, u32[]{:S(2)}) copy-start(f32[2,4]{1,0:T(2,128)} %param.8) | copy-start | bytes 100
  704.5 75.3 %copy-start.4 = (f32[2,4]{1,0:T(2,128)}, f32[2,4]{1,0:T(2,128)S(1)}, u32[]{:S(2)}) copy-start(f32[2,4]{1,0:T(2,128)S(1)} %get-tuple-element.6) | copy-start | bytes 100
Sparse Core Ops, SparseCore 0:
  187.9 154.9 reduce-scatter.1
  345.3 47.3 all-reduce.2
  395.4 87.0 all-gather.1
where the time goes:
time: 787 us; the launch traced here: 786 us
  waiting for transfers between devices  287 us (36%)
  other arithmetic  176 us (22%)
  blocking collectives  148 us (19%)
  local copies, waits for them, and re-layouts  141 us (18%)
  between operations  16.7 us (2%)
  matrix products  13.5 us (2%)
    scatter-add x1, other arithmetic, shards(): jax.ops.segment_sum(values, targets, num_segments=slot_count * cells)  170 us
    reduce_scatter x1, waiting for transfers between devices, shards(): owned = lax.psum_scatter(full_bins, 'det', scatter_dimension=0, tiled=True)  155 us
    all_gather x1, waiting for transfers between devices, shards(): whole_sky = lax.all_gather(sky_map, 'det', axis=0, tiled=True)  80.8 us
    psum x1, blocking collectives, shards(): lax.psum((jnp.sum(system_remainder * system_remainder), jnp.sum(conjugate...  74.6 us
    psum x1, blocking collectives, shards(): lax.psum(jnp.sum(updated_residual_vector * updated_residual_vector), ('tm...  73.4 us
    psum x1, waiting for transfers between devices, shards(): binned = lax.psum(owned, 'tm')  47.9 us
    gather x2, local copies, waits for them, and re-layouts, shards(): flat_sky[cell] + cos_weight * flat_sky[cell + WINDOW]  45.6 us
    gather x2, local copies, waits for them, and re-layouts, shards(): flat_sky[cell + WINDOW]  45.6 us
  transfers between devices with their start and end apart: 5, of which 4 were waited for; matrix products, arithmetic and copies ran while one was open for 0% of the time, Pallas kernels for 0%

commit v1 on v0

--- a/solution.py
+++ b/solution.py
@@ -108,8 +108,11 @@
         + stiffness * (2.0 * conjugate_heading - padded[:, :-2] - padded[:, 2:])
     )
     norm_now, curvature = lax.psum(
-        (jnp.sum(system_remainder * system_remainder), jnp.sum(conjugate_heading * applied)),
-        ("tm", "det"),
+        lax.psum(
+            (jnp.sum(system_remainder * system_remainder), jnp.sum(conjugate_heading * applied)),
+            "det",
+        ),
+        "tm",
     )
     conjugate_update_factor = norm_now / curvature
     updated_residual_vector = system_remainder - conjugate_update_factor * applied

time: 787 us -> 848 us (1.078)
  blocking collectives: 148 us -> 209 us
    psum x1, blocking collectives: 74.6 us -> 124 us  [shards(): lax.psum((jnp.sum(system_remainder * system_remainder), jnp.sum(conjugate...]
    psum x0 -> x1, blocking collectives: none -> 9.05 us  [shards(): lax.psum(lax.psum((jnp.sum(system_remainder * system_remainder), jnp.sum(...]
where the time goes in v1:
time: 848 us; the launch traced here: 847 us
  waiting for transfers between devices  287 us (34%)
  blocking collectives  209 us (25%)
  other arithmetic  176 us (21%)
  local copies, waits for them, and re-layouts  141 us (17%)
  between operations  16.7 us (2%)
  matrix products  13.5 us (2%)
    scatter-add x1, other arithmetic, shards(): jax.ops.segment_sum(values, targets, num_segments=slot_count * cells)  170 us
    reduce_scatter x1, waiting for transfers between devices, shards(): owned = lax.psum_scatter(full_bins, 'det', scatter_dimension=0, tiled=True)  155 us
    psum x1, blocking collectives, shards(): lax.psum((jnp.sum(system_remainder * system_remainder), jnp.sum(conjugate...  124 us
    all_gather x1, waiting for transfers between devices, shards(): whole_sky = lax.all_gather(sky_map, 'det', axis=0, tiled=True)  80.8 us
    psum x1, blocking collectives, shards(): lax.psum(jnp.sum(updated_residual_vector * updated_residual_vector), ('tm...  75.3 us
    psum x1, waiting for transfers between devices, shards(): binned = lax.psum(owned, 'tm')  47.9 us
    gather x2, local copies, waits for them, and re-layouts, shards(): flat_sky[cell] + cos_weight * flat_sky[cell + WINDOW]  45.6 us
    gather x2, local copies, waits for them, and re-layouts, shards(): flat_sky[cell + WINDOW]  45.6 us
  transfers between devices with their start and end apart: 5, of which 4 were waited for; matrix products, arithmetic and copies ran while one was open for 0% of the time, Pallas kernels for 0%

profile of v1, /device:TPU:1, one launch (start us, length us, event | category | flops | bytes accessed | tf_op | source)
XLA Modules:
  0.0 847.0 jit_solution(13214989791873277116)
XLA Ops:
  7.2 0.0 reduce-scatter.2.cloned.1.call-start
  7.2 0.7 broadcast_multiply_fusion
  7.9 0.1 broadcast_bitcast_fusion.2
  8.0 0.8 fusion.12
  8.9 0.8 broadcast_bitcast_fusion.1
  9.7 1.2 multiply_bitcast_fusion.1
  11.0 169.6 %scatter_custom_fusion = f32[98304]{0:T(1024)S(1)} fusion(s32[24576]{0:T(1024)S(1)} %pad_add_fusion, f32[24576]{0:T(1024)S(1)} %pad_maximum_fusion.1, f32[]{:T(128)} %constant.14.clone.1), kind=kCustom, calls=%fused_computation.10 | custom fusion | flops 24576 | bytes 393220 | tf_op jit(solution)/shard_map/scatter-add | solution.py:73
  180.6 0.1 reshape.67
  180.7 0.8 copy.13
  181.4 0.1 reshape_reshape.6
  181.6 0.0 copy-start
  181.6 6.2 fusion.1
  187.8 0.0 reduce-scatter.2.cloned.1.call-update
  187.8 0.0 all-reduce.4.cloned.1.call-start
  187.9 155.1 %reduce-scatter.2.cloned.1.call-done = f32[48,768]{1,0:T(8,128)} async-done(((f32[3072,768]{1,0:T(8,128)}), f32[48,768]{1,0:T(8,128)}) %reduce-scatter.2.cloned.1.call-update) | async-done | bytes 147472 | tf_op jit(solution)/shard_map/reduce_scatter | solution.py:86
  343.0 1.7 reshape.68
  344.6 0.0 all-reduce.4.cloned.1.call-update
  344.6 0.0 all-gather.2.cloned.1.call-start
  344.7 0.0 copy-done
  344.7 47.9 %all-reduce.4.cloned.1.call-done = f32[48,3,256]{2,1,0:T(4,128)} async-done(((f32[48,3,256]{2,1,0:T(4,128)}), f32[48,3,256]{2,1,0:T(4,128)}) %all-reduce.4.cloned.1.call-update) | async-done | bytes 147472 | tf_op jit(solution)/shard_map/psum | solution.py:87
  392.6 1.4 fusion.10
  394.1 0.1 pad_maximum_fusion
  394.2 0.7 copy.31
  394.9 0.0 all-gather.2.cloned.1.call-update
  394.9 0.0 copy-done.2
  394.9 0.1 fusion.17
  395.0 2.2 collective-permute-start
  397.2 1.3 collective-permute-start.1
  398.6 0.0 collective-permute-done
  398.6 3.0 collective-permute-done.1
  401.6 0.1 pad_maximum_fusion.2
  401.7 80.8 %all-gather.2.cloned.1.call-done = f32[3072,768]{1,0:T(8,128)} async-done(((f32[48,768]{1,0:T(8,128)}), f32[3072,768]{1,0:T(8,128)}) %all-gather.2.cloned.1.call-update) | async-done | bytes 9437200 | tf_op jit(solution)/shard_map/all_gather | solution.py:91
  482.5 7.3 fusion
  489.9 45.5 %gather_fusion = f32[8192]{0:T(1024)S(1)} fusion(f32[98304]{0:T(1024)S(1)} %reshape.70, s32[8192]{0:T(1024)S(1)} %broadcast_clamp_fusion.2), kind=kCustom, calls=%fused_computation | custom fusion | bytes 98304 | tf_op jit(solution)/shard_map/gather | solution.py:97
  535.4 45.5 %gather_fusion.1 = f32[8192]{0:T(1024)S(1)} fusion(f32[98304]{0:T(1024)S(1)} %reshape.70, s32[8192]{0:T(1024)S(1)} %broadcast_clamp_fusion.1), kind=kCustom, calls=%fused_computation.1 | custom fusion | bytes 98304 | tf_op jit(solution)/shard_map/gather | solution.py:98
  581.0 0.0 copy-start.1
  581.0 0.0 copy-start.3
  581.0 0.0 copy-start.5
  581.0 45.5 %gather_fusion.2 = f32[8192]{0:T(1024)S(1)} fusion(f32[98304]{0:T(1024)S(1)} %reshape.70, s32[8192]{0:T(1024)S(1)} %broadcast_clamp_fusion), kind=kCustom, calls=%fused_computation.2 | custom fusion | bytes 98304 | tf_op jit(solution)/shard_map/gather | solution.py:99
  626.6 0.0 copy-done.1
  626.6 0.5 multiply_add_fusion
  627.2 0.1 reduce_sum.37
  627.3 0.7 multiply_reduce_fusion.1
  627.9 124.3 %all-reduce = (f32[]{:T(128)}, f32[]{:T(128)}) all-reduce(f32[]{:T(128)} %get-tuple-element.36, f32[]{:T(128)} %get-tuple-element.9), channel_id=1, replica_groups=mesh['tm'=4,'det'=64] {'det'}, use_global_device_ids=true, to_apply=%region_1.2 | all-reduce | flops 2 | bytes 16 | tf_op jit(solution)/shard_map/psum | solution.py:111
  752.2 9.1 %all-reduce.1 = (f32[]{:T(128)}, f32[]{:T(128)}) all-reduce(f32[]{:T(128)} %get-tuple-element.3, f32[]{:T(128)} %get-tuple-element.4), channel_id=1, replica_groups=mesh['tm'=4,'det'=64] {'tm'}, use_global_device_ids=true, to_apply=%region_2.3 | all-reduce | flops 2 | bytes 16 | tf_op jit(solution)/shard_map/psum | solution.py:110
  762.6 0.6 multiply_reduce_fusion
  763.2 75.3 %psum.47 = f32[]{:T(128)} all-reduce(f32[]{:T(128)} %get-tuple-element.7), channel_id=1, replica_groups=mesh['tm'=4,'det'=64] {'tm','det'}, use_global_device_ids=true, to_apply=%region_11.12 | all-reduce | flops 1 | bytes 8 | tf_op jit(solution)/shard_map/psum | solution.py:119
  839.9 0.6 multiply_add_fusion.1
  (28 shorter events, 0.3 us)
Async XLA Ops:
  7.2 335.8 %reduce-scatter.2.cloned.1.call-start = ((), (), s32[]{:S(2)}) async-start(), calls=%async_computation.1 | async-start | bytes 9584640 | tf_op jit(solution)/shard_map/reduce_scatter | solution.py:86
  181.6 163.1 %copy-start = (f32[48,6,256]{2,0,1:T(8,128)S(1)}, f32[48,6,256]{2,0,1:T(8,128)}, u32[]{:S(2)}) copy-start(f32[48,6,256]{2,0,1:T(8,128)} %param.15) | copy-start | bytes 884740
  187.8 207.1 %copy-start.2 = (f32[2,4]{1,0:T(2,128)S(1)}, f32[2,4]{1,0:T(2,128)}, u32[]{:S(2)}) copy-start(f32[2,4]{1,0:T(2,128)} %param.10) | copy-start | bytes 100
  187.8 204.8 %all-reduce.4.cloned.1.call-start = ((), (), s32[]{:S(2)}) async-start(), calls=%async_computation.2 | async-start | bytes 393216 | tf_op jit(solution)/shard_map/psum | solution.py:87
  344.6 137.9 %all-gather.2.cloned.1.call-start = ((), (), s32[]{:S(2)}) async-start(), calls=%async_computation.3 | async-start | bytes 9584640 | tf_op jit(solution)/shard_map/all_gather | solution.py:91
  395.0 3.6 collective-permute-start
  397.2 4.4 collective-permute-start.1
  581.0 45.6 %copy-start.1 = (f32[2,4096]{1,0:T(2,128)S(1)}, f32[2,4096]{1,0:T(2,128)}, u32[]{:S(2)}) copy-start(f32[2,4096]{1,0:T(2,128)} %param.12) | copy-start | bytes 98308
  581.0 46.2 %copy-start.3 = (f32[2,4]{1,0:T(2,128)S(1)}, f32[2,4]{1,0:T(2,128)}, u32[]{:S(2)}) copy-start(f32[2,4]{1,0:T(2,128)} %param.9) | copy-start | bytes 100
  581.0 258.8 %copy-start.5 = (f32[2,4]{1,0:T(2,128)S(1)}, f32[2,4]{1,0:T(2,128)}, u32[]{:S(2)}) copy-start(f32[2,4]{1,0:T(2,128)} %param.8) | copy-start | bytes 100
  763.2 77.2 %copy-start.4 = (f32[2,4]{1,0:T(2,128)}, f32[2,4]{1,0:T(2,128)S(1)}, u32[]{:S(2)}) copy-start(f32[2,4]{1,0:T(2,128)S(1)} %get-tuple-element.8) | copy-start | bytes 100
Sparse Core Ops, SparseCore 0:
  187.9 154.9 reduce-scatter.1
  345.3 47.3 all-reduce.3
  395.4 87.0 all-gather.1
